TPU v7x, 256 devices: a whole 4x4x8 slice. The times are simulated.
256 devices in a mesh: energy: 64 (over x, z_hi, y), space: 4 (over z_lo, core).
Axes of the slice: x: 4, y: 4, z: 8 (z_hi: 4, z_lo: 2; z = z_hi * 2 + z_lo), core: 2. Of those that a mesh axis runs over, the one named last changes fastest.
Arguments:
- g_lesser: bfloat16 [64, 2, 4, 512, 512], P('energy', None, 'space'), may hold values from -6 to 6, as said below
- w_lesser: bfloat16 [64, 2, 4, 512, 512], P('energy', None, 'space'), may hold values from -6 to 6, as said below
- g_retarded: bfloat16 [64, 2, 4, 4, 512, 512], P('energy', None, 'space'), may hold values from -0.1875 to 0.1875
- energy_index: int32 [64], replicated, may hold values from 0 to 63, each once
Outputs:
- sigma_lesser: bfloat16 [64, 2, 4, 512, 512], P('energy', None, 'space')
- delta_green: bfloat16 [64, 2, 4, 512, 512], P('energy', None, 'space')
Inputs may be any that keep to these rules, and one draw needn't show every extreme that they name: `g_lesser`: anti-Hermitian in every diagonal block at every energy: element (j, i) of component 0 is minus element (i, j), of component 1 equal to it. `w_lesser`: anti-Hermitian in every diagonal block at every energy: element (j, i) of component 0 is minus element (i, j), of component 1 equal to it. `energy_index`: each grid point once.
All inputs are finite; a program needn't handle non-finite values.
Results may differ from a plain program's by a relative error of at most 0.013.
Values may be sent and summed in bfloat16 or wider, within the bound.
A program may use at most 128 MiB of HBM per device.

v0:
```python
import math
import jax
import jax.numpy as jnp
from jax import lax
from jax.sharding import PartitionSpec as P


def twiddles(energy_index, per_device, groups):
    grid_size = energy_index.shape[0]
    padded_len = 2 * grid_size
    row_count = 2 * grid_size
    row_ids = lax.iota(jnp.int32, row_count)
    local_energy = row_ids // (2 * groups)
    component = row_ids // groups % 2
    source = row_ids % groups
    stored = source * per_device + local_energy
    grid_point = energy_index[stored]
    frequency = lax.iota(jnp.int32, padded_len)
    forward_phase = frequency[:, None] * grid_point[None, :] % padded_len
    forward_angle = forward_phase.astype(jnp.float32) * (2.0 * math.pi / padded_len)
    cos_fwd = jnp.cos(forward_angle)
    sin_fwd = jnp.sin(forward_angle)
    real_column = (component == 0)[None, :]
    forward = jnp.concatenate(
        [jnp.where(real_column, cos_fwd, sin_fwd), jnp.where(real_column, -sin_fwd, cos_fwd)],
        axis=0,
    )
    shifted = grid_point + grid_size // 2
    backward_phase = shifted[:, None] * frequency[None, :] % padded_len
    backward_angle = backward_phase.astype(jnp.float32) * (2.0 * math.pi / padded_len)
    cos_back = jnp.cos(backward_angle)
    sin_back = jnp.sin(backward_angle)
    real_row = (component == 0)[:, None]
    factor = grid_size ** (-0.5) / padded_len
    left_half = jnp.where(real_row, -sin_back, cos_back) * factor
    right_half = jnp.where(real_row, -cos_back, -sin_back) * factor
    backward = jnp.concatenate([left_half, right_half], axis=1)
    return (forward, backward)


def transform(matrix_high, matrix_low, operand):
    return jnp.dot(matrix_high, operand, preferred_element_type=jnp.float32) + jnp.dot(
        matrix_low, operand, preferred_element_type=jnp.float32
    )


def convolve(green_rows, screen_rows, forward, backward):
    padded_len = forward.shape[0] // 2
    forward_high = forward.astype(jnp.bfloat16)
    forward_low = (forward - forward_high.astype(jnp.float32)).astype(jnp.bfloat16)
    green_hat = transform(forward_high, forward_low, green_rows)
    screen_hat = transform(forward_high, forward_low, screen_rows)
    green_real = green_hat[:padded_len]
    green_imag = green_hat[padded_len:]
    screen_real = screen_hat[:padded_len]
    screen_imag = screen_hat[padded_len:]
    prod_real = green_real * screen_real - green_imag * screen_imag
    prod_imag = green_real * screen_imag + green_imag * screen_real
    merged = jnp.concatenate([prod_real, prod_imag], axis=0)
    return jnp.dot(backward, merged, precision=lax.Precision.HIGH).astype(jnp.bfloat16)


def shards(g_lesser, w_lesser, g_retarded, energy_index):
    energies_here = g_lesser.shape[0]
    width = g_lesser.shape[3]
    groups = lax.axis_size("energy")
    forward, backward = twiddles(energy_index, energies_here, groups)
    own_row = g_retarded[:, :, 0]
    columns = width * width // groups
    green = g_lesser.reshape(energies_here, 2, groups, columns)
    screen = w_lesser.reshape(energies_here, 2, groups, columns)
    green_el, screen_el = (
        lax.all_to_all(green, "energy", split_axis=2, concat_axis=2, tiled=True),
        lax.all_to_all(screen, "energy", split_axis=2, concat_axis=2, tiled=True),
    )
    sigma_el = convolve(
        green_el.reshape(-1, columns), screen_el.reshape(-1, columns), forward, backward
    )
    sigma_el = sigma_el.reshape(energies_here, 2, groups, columns)
    sigma_back = lax.all_to_all(sigma_el, "energy", split_axis=2, concat_axis=2, tiled=True)
    sigma_lesser = sigma_back.reshape(energies_here, 2, 1, width, width)
    first_prod = jnp.einsum(
        "ecnij,ednjl->encdil",
        own_row,
        lax.all_gather(sigma_lesser, "space", axis=2, tiled=True),
        preferred_element_type=jnp.float32,
    )
    left_product = jnp.stack(
        [
            first_prod[:, :, 0, 0] - first_prod[:, :, 1, 1],
            first_prod[:, :, 0, 1] + first_prod[:, :, 1, 0],
        ],
        axis=1,
    ).astype(jnp.bfloat16)
    second_prod = jnp.einsum(
        "ecnil,ednml->ecdim", left_product, own_row, preferred_element_type=jnp.float32
    )
    out_real = second_prod[:, 0, 0] + second_prod[:, 1, 1]
    out_imag = second_prod[:, 1, 0] - second_prod[:, 0, 1]
    delta = jnp.stack([out_real, out_imag], axis=1)
    delta_green = delta.astype(jnp.bfloat16).reshape(energies_here, 2, 1, width, width)
    return (sigma_lesser, delta_green)


def solution(mesh):
    return jax.shard_map(
        shards,
        mesh=mesh,
        in_specs=(
            P("energy", None, "space", None, None),
            P("energy", None, "space", None, None),
            P("energy", None, "space", None, None, None),
            P(),
        ),
        out_specs=(P("energy", None, "space", None, None), P("energy", None, "space", None, None)),
        check_vma=False,
    )
```

profile of v0, /device:TPU:1, one launch (start us, length us, event | category | flops | bytes accessed | tf_op | source)
XLA Modules:
  0.0 215.1 jit_solution(1046797866290290498)
XLA Ops:
  7.2 0.0 copy-start
  7.2 0.0 copy-start.4
  7.2 1.6 reshape.274
  8.8 2.1 copy.28
  10.9 15.1 %all-to-all-start.1 = ((bf16[1,2,64,4096]{3,1,0,2:T(2,128)(2,1)}), bf16[1,2,64,4096]{3,1,0,2:T(2,128)(2,1)S(1)}, u32[]{:S(2)}, u32[]{:S(2)}) async-start(bf16[1,2,64,4096]{3,1,0,2:T(2,128)(2,1)} %copy.28), calls=%async_computation.1 | async-start | bytes 2097152 | tf_op jit(solution)/shard_map/all_to_all | solution.py:74
  26.0 0.0 copy-done.4
  26.0 0.5 reshape.272
  26.6 2.1 copy.26
  28.6 25.1 %all-to-all-done.1 = bf16[1,2,64,4096]{3,1,0,2:T(2,128)(2,1)S(1)} async-done(((bf16[1,2,64,4096]{3,1,0,2:T(2,128)(2,1)}), bf16[1,2,64,4096]{3,1,0,2:T(2,128)(2,1)S(1)}, u32[]{:S(2)}, u32[]{:S(2)}) %all-to-all-start.1) | async-done | bytes 1048608 | tf_op jit(solution)/shard_map/all_to_all | solution.py:74
  53.7 8.3 %all-to-all-start = ((bf16[1,2,64,4096]{3,1,0,2:T(2,128)(2,1)}), bf16[1,2,64,4096]{3,1,0,2:T(2,128)(2,1)S(1)}, u32[]{:S(2)}, u32[]{:S(2)}) async-start(bf16[1,2,64,4096]{3,1,0,2:T(2,128)(2,1)} %copy.26), calls=%async_computation | async-start | bytes 2097152 | tf_op jit(solution)/shard_map/all_to_all | solution.py:73
  62.0 0.2 all-gather.2.cloned.1.call-start
  62.3 0.0 copy-done
  62.3 1.2 gather_fusion
  63.6 0.6 select_multiply_fusion.1
  64.2 0.6 copy.29
  64.8 0.7 fusion.36
  65.5 2.6 %convolution_add_fusion = f32[256,4096]{1,0:T(8,128)} fusion(f32[256,4096]{1,0:T(8,128)S(1)} %fusion.36, bf16[128,4096]{1,0:T(8,128)(2,1)S(1)} %bitcast.74, f32[128,128]{1,0:T(8,128)S(1)} %get-tuple-element.18, f32[128,128]{1,0:T(8,128)S(1)} %get-tuple-element.19), kind=kOutput, calls=%fused_computation.2 | convolution fusion | flops 269647872 | bytes 9568256 | tf_op jit(solution)/shard_map/dot_general | solution.py:42
  68.1 22.7 %all-to-all-done = bf16[1,2,64,4096]{3,1,0,2:T(2,128)(2,1)S(1)} async-done(((bf16[1,2,64,4096]{3,1,0,2:T(2,128)(2,1)}), bf16[1,2,64,4096]{3,1,0,2:T(2,128)(2,1)S(1)}, u32[]{:S(2)}, u32[]{:S(2)}) %all-to-all-start) | async-done | bytes 1048608 | tf_op jit(solution)/shard_map/all_to_all | solution.py:73
  90.8 0.6 copy.27
  91.3 0.7 fusion.38
  92.0 0.0 copy-start.2
  92.0 0.7 convolution_add_fusion.1
  92.8 1.5 copy-done.2
  94.2 0.9 multiply_subtract_fusion
  95.2 1.5 convolution_convert_fusion
  96.7 1.1 copy.30
  97.8 32.1 %all_to_all.15 = bf16[1,2,64,4096]{3,1,0,2:T(2,128)(2,1)S(1)} all-to-all(bf16[1,2,64,4096]{3,1,0,2:T(2,128)(2,1)S(1)} %copy.30), channel_id=1, replica_groups=mesh['energy'=64,'space'=4] {'energy'}, dimensions={2} | all-to-all | bytes 2097152 | tf_op jit(solution)/shard_map/all_to_all | solution.py:80
  130.0 0.6 copy.31
  130.6 1.3 reshape.277
  131.9 0.0 all-gather.2.cloned.1.call-update
  131.9 47.4 %all-gather.2.cloned.1.call-done = bf16[1,2,4,512,512]{4,3,1,0,2:T(8,128)(2,1)} async-done(((bf16[1,2,1,512,512]{4,3,1,0,2:T(8,128)(2,1)}), bf16[1,2,4,512,512]{4,3,1,0,2:T(8,128)(2,1)}) %all-gather.2.cloned.1.call-update) | async-done | bytes 4194320 | tf_op jit(solution)/shard_map/all_gather | solution.py:85
  179.3 14.1 %convolution_bitcast_fusion = f32[1,4,2,2,512,512]{4,5,2,3,1,0:T(8,128)} fusion(bf16[1,2,4,512,512]{4,3,1,0,2:T(8,128)(2,1)} %all-gather.2.cloned.1.call-done, bf16[1,2,1,4,512,512]{5,4,3,2,1,0:T(8,128)(2,1)} %param.6), kind=kOutput, calls=%fused_computation.1 | convolution fusion | flops 4294967296 | bytes 25165824 | tf_op jit(solution)/shard_map/ecnij,ednjl->encdil/dot_general | solution.py:82
  193.4 4.2 %fusion.13 = bf16[1,4,512,512]{2,3,1,0:T(8,128)(2,1)S(1)} fusion(f32[1,4,2,2,512,512]{4,5,2,3,1,0:T(8,128)} %convolution_bitcast_fusion), kind=kLoop, calls=%fused_computation.22 | loop fusion | flops 2097152 | bytes 10485760 | tf_op jit(solution)/shard_map/add | solution.py:91
  197.6 0.0 copy-start.3
  197.6 4.4 %fusion.12 = bf16[1,4,512,512]{2,3,1,0:T(8,128)(2,1)S(1)} fusion(f32[1,4,2,2,512,512]{4,5,2,3,1,0:T(8,128)} %convolution_bitcast_fusion), kind=kLoop, calls=%fused_computation.21 | loop fusion | flops 2097152 | bytes 10485760 | tf_op jit(solution)/shard_map/sub | solution.py:90
  202.1 0.2 copy-done.3
  202.3 0.0 copy-start.1
  202.3 4.5 %fusion.11 = f32[1,2,2,512,512]{4,3,2,1,0:T(8,128)S(1)} fusion(bf16[1,4,512,512]{2,3,1,0:T(8,128)(2,1)S(1)} %fusion.13, bf16[1,4,512,512]{2,3,1,0:T(8,128)(2,1)S(1)} %fusion.12, bf16[1,2,1,4,512,512]{5,4,3,2,1,0:T(8,128)(2,1)S(1)} %copy-done.3), kind=kOutput, calls=%fused_computation.20 | convolution fusion | flops 4303355904 | bytes 12582912 | tf_op jit(solution)/shard_map/ecnil,ednml->ecdim/dot_general | solution.py:95
  206.8 0.4 fusion.15
  207.2 1.1 pad_maximum_fusion
  208.2 0.0 copy-done.1
  (4 shorter events, 0.0 us)
Async XLA Ops:
  7.2 55.1 %copy-start = (s32[64]{0:T(128)S(1)}, s32[64]{0:T(128)}, u32[]{:S(2)}) copy-start(s32[64]{0:T(128)} %param.7) | copy-start | bytes 772
  7.2 18.8 %copy-start.4 = (bf16[1,2,1,512,512]{4,3,2,1,0:T(8,128)(2,1)S(1)}, bf16[1,2,1,512,512]{4,3,2,1,0:T(8,128)(2,1)}, u32[]{:S(2)}) copy-start(bf16[1,2,1,512,512]{4,3,2,1,0:T(8,128)(2,1)} %param.4) | copy-start | bytes 3145732
  10.9 42.8 %all-to-all-start.1 = ((bf16[1,2,64,4096]{3,1,0,2:T(2,128)(2,1)}), bf16[1,2,64,4096]{3,1,0,2:T(2,128)(2,1)S(1)}, u32[]{:S(2)}, u32[]{:S(2)}) async-start(bf16[1,2,64,4096]{3,1,0,2:T(2,128)(2,1)} %copy.28), calls=%async_computation.1 | async-start | bytes 2097152 | tf_op jit(solution)/shard_map/all_to_all | solution.py:74
  53.7 37.0 %all-to-all-start = ((bf16[1,2,64,4096]{3,1,0,2:T(2,128)(2,1)}), bf16[1,2,64,4096]{3,1,0,2:T(2,128)(2,1)S(1)}, u32[]{:S(2)}, u32[]{:S(2)}) async-start(bf16[1,2,64,4096]{3,1,0,2:T(2,128)(2,1)} %copy.26), calls=%async_computation | async-start | bytes 2097152 | tf_op jit(solution)/shard_map/all_to_all | solution.py:73
  62.0 117.3 %all-gather.2.cloned.1.call-start = ((), (), s32[]{:S(2)}) async-start(), calls=%async_computation.3 | async-start | bytes 5242880 | tf_op jit(solution)/shard_map/all_gather | solution.py:85
  92.0 2.2 %copy-start.2 = (f32[256,4096]{1,0:T(8,128)S(1)}, f32[256,4096]{1,0:T(8,128)}, u32[]{:S(2)}) copy-start(f32[256,4096]{1,0:T(8,128)} %convolution_add_fusion) | copy-start | bytes 12582916
  197.6 4.6 %copy-start.3 = (bf16[1,2,1,4,512,512]{5,4,3,2,1,0:T(8,128)(2,1)S(1)}, bf16[1,2,1,4,512,512]{5,4,3,2,1,0:T(8,128)(2,1)}, u32[]{:S(2)}) copy-start(bf16[1,2,1,4,512,512]{5,4,3,2,1,0:T(8,128)(2,1)} %param.6) | copy-start | bytes 12582916
  202.3 6.0 %copy-start.1 = (s32[64]{0:T(128)S(1)}, s32[64]{0:T(128)}, u32[]{:S(2)}) copy-start(s32[64]{0:T(128)} %param.7) | copy-start | bytes 772
Sparse Core Ops, SparseCore 0:
  132.0 47.2 all-gather.1
where the time goes:
time: 215 us
  waiting for transfers between devices  95.2 us (44%)
  blocking collectives  32.1 us (15%)
  matrix products  24.9 us (12%)
  starting transfers between devices  23.7 us (11%)
  between operations  14.2 us (7%)
  local copies, waits for them, and re-layouts  13.4 us (6%)
  other arithmetic  11.6 us (5%)
    all_gather x1, waiting for transfers between devices, shards(): lax.all_gather(sigma_lesser, 'space', axis=2, tiled=True)  47.4 us
    all_to_all x1, blocking collectives, shards(): lax.all_to_all(sigma_el, 'energy', split_axis=2, concat_axis=2, tiled=True)  32.1 us
    all_to_all x1, waiting for transfers between devices, shards(): lax.all_to_all(screen, 'energy', split_axis=2, concat_axis=2, tiled=True)  25.1 us
    all_to_all x1, waiting for transfers between devices, shards(): lax.all_to_all(green, 'energy', split_axis=2, concat_axis=2, tiled=True)  22.7 us
    all_to_all x1, starting transfers between devices, shards(): lax.all_to_all(screen, 'energy', split_axis=2, concat_axis=2, tiled=True)  15.1 us
    dot_general x1, matrix products, shards(): jnp.einsum('ecnij,ednjl->encdil', own_row, lax.all_gather(sigma_lesser, '...  14.1 us
    all_to_all x1, starting transfers between devices, shards(): lax.all_to_all(green, 'energy', split_axis=2, concat_axis=2, tiled=True)  8.33 us
    dot_general x1, matrix products, shards(): jnp.einsum('ecnil,ednml->ecdim', left_product, own_row, preferred_element...  4.54 us
  transfers between devices with their start and end apart: 3, of which 3 were waited for; matrix products, arithmetic and copies ran while one was open for 4% of the time, Pallas kernels for 0%

commit v1 on v0

--- a/solution.py
+++ b/solution.py
@@ -70,7 +70,12 @@
     green = g_lesser.reshape(energies_here, 2, groups, columns)
     screen = w_lesser.reshape(energies_here, 2, groups, columns)
     green_el, screen_el = (
-        lax.all_to_all(green, "energy", split_axis=2, concat_axis=2, tiled=True),
+        jnp.concatenate(
+            lax.all_to_all(
+                jnp.stack(jnp.split(green, lax.axis_size("energy"), axis=2)), "energy", 0, 0
+            ),
+            axis=2,
+        ),
         lax.all_to_all(screen, "energy", split_axis=2, concat_axis=2, tiled=True),
     )
     sigma_el = convolve(

time: 215 us -> 265 us (1.23)
  local copies, waits for them, and re-layouts: 13.4 us -> 58.7 us
  waiting for transfers between devices: 95.2 us -> 98.3 us
    unnamed x10 -> x69, local copies, waits for them, and re-layouts: 1.71 us -> 39.8 us
    all_to_all x1, starting transfers between devices: 8.33 us -> 15.1 us  [shards(): lax.all_to_all(jnp.stack(jnp.split(green, lax.axis_size('energy'), axis=2...]
    all_to_all x1, starting transfers between devices: 15.1 us -> 8.33 us  [shards(): lax.all_to_all(screen, 'energy', split_axis=2, concat_axis=2, tiled=True)]
    add x1 -> x0, other arithmetic: 4.19 us -> none  [shards(): first_prod[:, :, 0, 1] + first_prod[:, :, 1, 0]]
    sub x0 -> x1, local copies, waits for them, and re-layouts: none -> 4.15 us  [shards(): first_prod[:, :, 0, 0] - first_prod[:, :, 1, 1]]
    sub x1, other arithmetic: 4.42 us -> 8 us  [shards(): first_prod[:, :, 0, 0] - first_prod[:, :, 1, 1]]
    dot_general x1, matrix products: 4.54 us -> 7.68 us  [shards(): jnp.einsum('ecnil,ednml->ecdim', left_product, own_row, preferred_element...]
  transfers between devices with their start and end apart: 3 -> 3, of which waited for: 3 -> 3; matrix products, arithmetic and copies ran while one was open for 4% -> 2% of each run, Pallas kernels for 0% -> 0%
where the time goes in v1:
time: 265 us; the launch traced here: 264 us
  waiting for transfers between devices  98.3 us (37%)
  local copies, waits for them, and re-layouts  58.7 us (22%)
  blocking collectives  32.5 us (12%)
  matrix products  26.1 us (10%)
  starting transfers between devices  23.7 us (9%)
  between operations  14.3 us (5%)
  other arithmetic  11 us (4%)
    all_gather x1, waiting for transfers between devices, shards(): lax.all_gather(sigma_lesser, 'space', axis=2, tiled=True)  47.2 us
    unnamed x69, local copies, waits for them, and re-layouts  39.8 us
    all_to_all x1, blocking collectives, shards(): lax.all_to_all(sigma_el, 'energy', split_axis=2, concat_axis=2, tiled=True)  32.5 us
    all_to_all x1, waiting for transfers between devices, shards(): lax.all_to_all(screen, 'energy', split_axis=2, concat_axis=2, tiled=True)  26 us
    all_to_all x1, waiting for transfers between devices, shards(): lax.all_to_all(jnp.stack(jnp.split(green, lax.axis_size('energy'), axis=2...  25.1 us
    all_to_all x1, starting transfers between devices, shards(): lax.all_to_all(jnp.stack(jnp.split(green, lax.axis_size('energy'), axis=2...  15.1 us
    dot_general x1, matrix products, shards(): jnp.einsum('ecnij,ednjl->encdil', own_row, lax.all_gather(sigma_lesser, '...  14.1 us
    all_to_all x1, starting transfers between devices, shards(): lax.all_to_all(screen, 'energy', split_axis=2, concat_axis=2, tiled=True)  8.33 us
  transfers between devices with their start and end apart: 3, of which 3 were waited for; matrix products, arithmetic and copies ran while one was open for 2% of the time, Pallas kernels for 0%

profile of v1, /device:TPU:1, one launch (start us, length us, event | category | flops | bytes accessed | tf_op | source)
XLA Modules:
  0.0 264.5 jit_solution(10439636351570674599)
XLA Ops:
  7.2 1.6 reshape.272
  9.0 0.7 fusion.50
  9.7 0.7 fusion.48
  10.9 0.6 constant_dynamic-update-slice_fusion.63
  11.6 0.6 constant_dynamic-update-slice_fusion.62
  12.2 0.6 constant_dynamic-update-slice_fusion.61
  12.8 0.6 constant_dynamic-update-slice_fusion.60
  13.5 0.6 constant_dynamic-update-slice_fusion.59
  14.1 0.6 constant_dynamic-update-slice_fusion.58
  14.7 0.6 constant_dynamic-update-slice_fusion.57
  15.4 0.6 constant_dynamic-update-slice_fusion.56
  16.6 0.6 constant_dynamic-update-slice_fusion.54
  17.3 0.6 constant_dynamic-update-slice_fusion.53
  17.9 0.6 constant_dynamic-update-slice_fusion.52
  18.5 0.6 constant_dynamic-update-slice_fusion.51
  19.2 0.6 constant_dynamic-update-slice_fusion.50
  19.8 0.6 constant_dynamic-update-slice_fusion.49
  20.4 0.6 constant_dynamic-update-slice_fusion.48
  21.1 0.6 constant_dynamic-update-slice_fusion.47
  21.7 0.6 constant_dynamic-update-slice_fusion.46
  22.3 0.6 constant_dynamic-update-slice_fusion.45
  22.9 0.6 constant_dynamic-update-slice_fusion.44
  23.6 0.6 constant_dynamic-update-slice_fusion.43
  24.2 0.6 constant_dynamic-update-slice_fusion.42
  24.8 0.6 constant_dynamic-update-slice_fusion.41
  25.5 0.6 constant_dynamic-update-slice_fusion.40
  26.1 0.6 constant_dynamic-update-slice_fusion.39
  26.7 0.6 constant_dynamic-update-slice_fusion.38
  27.4 0.6 constant_dynamic-update-slice_fusion.37
  28.6 0.6 constant_dynamic-update-slice_fusion.35
  29.3 0.6 constant_dynamic-update-slice_fusion.34
  29.9 0.6 constant_dynamic-update-slice_fusion.33
  30.5 0.6 constant_dynamic-update-slice_fusion.32
  31.2 0.6 constant_dynamic-update-slice_fusion.31
  31.8 0.6 constant_dynamic-update-slice_fusion.30
  32.4 0.6 constant_dynamic-update-slice_fusion.29
  33.1 0.6 constant_dynamic-update-slice_fusion.28
  33.7 0.6 constant_dynamic-update-slice_fusion.27
  34.3 0.6 constant_dynamic-update-slice_fusion.26
  35.0 0.6 constant_dynamic-update-slice_fusion.25
  35.6 0.6 constant_dynamic-update-slice_fusion.24
  36.2 0.6 constant_dynamic-update-slice_fusion.23
  51.4 15.1 %all-to-all-start = ((bf16[64,1,2,1,4096]{4,2,3,1,0:T(2,128)(2,1)}), bf16[64,1,2,1,4096]{4,2,3,1,0:T(2,128)(2,1)S(1)}, u32[]{:S(2)}, u32[]{:S(2)}) async-start(bf16[64,1,2,1,4096]{4,2,3,1,0:T(2,128)(2,1)} %constant_dynamic-update-slice_fusion), calls=%async_computation | async-start | bytes 2097152 | tf_op jit(solution)/shard_map/all_to_all | solution.py:74
  67.0 2.1 copy.1683
  69.1 25.1 %all-to-all-done = bf16[64,1,2,1,4096]{4,2,3,1,0:T(2,128)(2,1)S(1)} async-done(((bf16[64,1,2,1,4096]{4,2,3,1,0:T(2,128)(2,1)}), bf16[64,1,2,1,4096]{4,2,3,1,0:T(2,128)(2,1)S(1)}, u32[]{:S(2)}, u32[]{:S(2)}) %all-to-all-start) | async-done | bytes 1048608 | tf_op jit(solution)/shard_map/all_to_all | solution.py:74
  94.2 8.3 %all-to-all-start.1 = ((bf16[1,2,64,4096]{3,1,0,2:T(2,128)(2,1)}), bf16[1,2,64,4096]{3,1,0,2:T(2,128)(2,1)S(1)}, u32[]{:S(2)}, u32[]{:S(2)}) async-start(bf16[1,2,64,4096]{3,1,0,2:T(2,128)(2,1)} %copy.1683), calls=%async_computation.1 | async-start | bytes 2097152 | tf_op jit(solution)/shard_map/all_to_all | solution.py:79
  102.8 1.2 gather_fusion
  105.2 26.0 %all-to-all-done.1 = bf16[1,2,64,4096]{3,1,0,2:T(2,128)(2,1)S(1)} async-done(((bf16[1,2,64,4096]{3,1,0,2:T(2,128)(2,1)}), bf16[1,2,64,4096]{3,1,0,2:T(2,128)(2,1)S(1)}, u32[]{:S(2)}, u32[]{:S(2)}) %all-to-all-start.1) | async-done | bytes 1048608 | tf_op jit(solution)/shard_map/all_to_all | solution.py:79
  131.8 0.7 fusion.35
  132.5 0.7 convolution_add_fusion
  133.2 0.7 fusion.37
  133.9 0.7 convolution_add_fusion.1
  134.7 0.9 multiply_subtract_fusion
  135.6 1.5 convolution_convert_fusion
  137.2 1.1 copy.1685
  138.3 32.5 %all_to_all.15 = bf16[1,2,64,4096]{3,1,0,2:T(2,128)(2,1)S(1)} all-to-all(bf16[1,2,64,4096]{3,1,0,2:T(2,128)(2,1)S(1)} %copy.1685), channel_id=1, replica_groups=mesh['energy'=64,'space'=4] {'energy'}, dimensions={2} | all-to-all | bytes 2097152 | tf_op jit(solution)/shard_map/all_to_all | solution.py:85
  171.3 1.3 reshape.277
  172.7 47.2 %all-gather.2.cloned.1.call-done = bf16[1,2,4,512,512]{4,3,1,0,2:T(8,128)(2,1)} async-done(((bf16[1,2,1,512,512]{4,3,1,0,2:T(8,128)(2,1)}), bf16[1,2,4,512,512]{4,3,1,0,2:T(8,128)(2,1)}) %all-gather.2.cloned.1.call-update) | async-done | bytes 4194320 | tf_op jit(solution)/shard_map/all_gather | solution.py:90
  219.8 14.1 %convolution_bitcast_fusion = f32[1,4,2,2,512,512]{4,5,2,3,1,0:T(8,128)} fusion(bf16[1,2,4,512,512]{4,3,1,0,2:T(8,128)(2,1)} %all-gather.2.cloned.1.call-done, bf16[1,2,1,4,512,512]{5,4,3,2,1,0:T(8,128)(2,1)} %param.6), kind=kOutput, calls=%fused_computation.1 | convolution fusion | flops 4294967296 | bytes 25165824 | tf_op jit(solution)/shard_map/ecnij,ednjl->encdil/dot_general | solution.py:87
  233.9 8.0 %fusion.11 = (bf16[1,4,512,512]{2,3,1,0:T(8,128)(2,1)}, bf16[1,4,512,512]{2,3,1,0:T(8,128)(2,1)S(1)}) fusion(f32[1,4,2,2,512,512]{4,5,2,3,1,0:T(8,128)} %convolution_bitcast_fusion), kind=kLoop, calls=%fused_computation.19 | loop fusion | flops 4194304 | bytes 20971520 | tf_op jit(solution)/shard_map/sub | solution.py:95
  241.9 4.2 %copy.1690 = bf16[1,4,512,512]{3,2,1,0:T(8,128)(2,1)} copy(bf16[1,4,512,512]{2,3,1,0:T(8,128)(2,1)} %get-tuple-element.68) | data formatting | bytes 4194304 | tf_op jit(solution)/shard_map/sub | solution.py:95
  246.1 2.4 copy.1691
  248.5 7.7 %fusion.10 = f32[1,2,2,512,512]{4,3,2,1,0:T(8,128)S(1)} fusion(bf16[1,4,512,512]{3,2,1,0:T(8,128)(2,1)} %copy.1691, bf16[1,4,512,512]{3,2,1,0:T(8,128)(2,1)} %copy.1690, bf16[1,2,1,4,512,512]{5,4,3,2,1,0:T(8,128)(2,1)} %param.6), kind=kOutput, calls=%fused_computation.18 | convolution fusion | flops 4303355904 | bytes 12582912 | tf_op jit(solution)/shard_map/ecnil,ednml->ecdim/dot_general | solution.py:100
  256.5 1.1 pad_maximum_fusion
  (45 shorter events, 20.1 us)
Async XLA Ops:
  7.2 95.6 %copy-start = (s32[64]{0:T(128)S(1)}, s32[64]{0:T(128)}, u32[]{:S(2)}) copy-start(s32[64]{0:T(128)} %param.7) | copy-start | bytes 772
  9.6 56.9 %copy-start.2 = (bf16[1,2,1,512,512]{4,3,2,1,0:T(8,128)(2,1)S(1)}, bf16[1,2,1,512,512]{4,3,2,1,0:T(8,128)(2,1)}, u32[]{:S(2)}) copy-start(bf16[1,2,1,512,512]{4,3,2,1,0:T(8,128)(2,1)} %param.5) | copy-start | bytes 3145732
  51.4 42.8 %all-to-all-start = ((bf16[64,1,2,1,4096]{4,2,3,1,0:T(2,128)(2,1)}), bf16[64,1,2,1,4096]{4,2,3,1,0:T(2,128)(2,1)S(1)}, u32[]{:S(2)}, u32[]{:S(2)}) async-start(bf16[64,1,2,1,4096]{4,2,3,1,0:T(2,128)(2,1)} %constant_dynamic-update-slice_fusion), calls=%async_computation | async-start | bytes 2097152 | tf_op jit(solution)/shard_map/all_to_all | solution.py:74
  94.2 37.0 %all-to-all-start.1 = ((bf16[1,2,64,4096]{3,1,0,2:T(2,128)(2,1)}), bf16[1,2,64,4096]{3,1,0,2:T(2,128)(2,1)S(1)}, u32[]{:S(2)}, u32[]{:S(2)}) async-start(bf16[1,2,64,4096]{3,1,0,2:T(2,128)(2,1)} %copy.1683), calls=%async_computation.1 | async-start | bytes 2097152 | tf_op jit(solution)/shard_map/all_to_all | solution.py:79
  102.5 117.3 %all-gather.2.cloned.1.call-start = ((), (), s32[]{:S(2)}) async-start(), calls=%async_computation.3 | async-start | bytes 5242880 | tf_op jit(solution)/shard_map/all_gather | solution.py:90
  248.5 9.1 %copy-start.1 = (s32[64]{0:T(128)S(1)}, s32[64]{0:T(128)}, u32[]{:S(2)}) copy-start(s32[64]{0:T(128)} %param.7) | copy-start | bytes 772
Sparse Core Ops, SparseCore 0:
  172.8 47.0 all-gather.1
